TPU v7x, 128 devices: a whole 4x4x4 slice. The times are simulated.
128 devices in a mesh: seq: 32 (over y, x, core), hid: 4 (over z).
Axes of the slice: x: 4, y: 4, z: 4, core: 2. Of those that a mesh axis runs over, the one named last changes fastest.
Arguments:
- patches: bfloat16 [12288, 3200], P('seq'), may hold values from -6 to 6
- norm_gain: float32 [3200], replicated, may hold values from 0.5 to 8
- query_weight: bfloat16 [3200, 2048], P(None, 'hid'), may hold values from -0.109375 to 0.109375
- key_weight: bfloat16 [3200, 2048], P(None, 'hid'), may hold values from -0.7424621 to 0.7424621
- value_weight: bfloat16 [3200, 2048], P(None, 'hid'), may hold values from -0.109375 to 0.109375
- out_weight: bfloat16 [2048, 3200], P('hid'), may hold values from -0.125 to 0.125
- layer_scale: float32 [3200], replicated, may hold values from 0.3 to 1.5
- merge_gain: float32 [12800], P('hid'), may hold values from 0.5 to 1.5
- merge_bias: float32 [12800], P('hid'), may hold values from -3 to 3
- proj_weight: bfloat16 [12800, 6144], P('hid', 'seq'), may hold values from -0.0546875 to 0.0546875
- proj_bias: float32 [6144], P('seq'), may hold values from -3 to 3
- text_rows: bfloat16 [512, 6144], P(None, 'seq'), may hold values from -6 to 6
- stream_gain: float32 [6144], P('hid'), may hold values from 0.5 to 1.5
- tile_counts: int32 [3], replicated, may hold values from 1 to 7, as said below
- image_slots: int32 [3072], replicated, may hold values from 0 to 3583, as said below
- text_slots: int32 [512], replicated, may hold values from 0 to 3583, as said below
Outputs:
- stream: bfloat16 [3584, 6144], P('seq', 'hid')
- normed: bfloat16 [3584, 6144], P('seq', 'hid')
Inputs may be any that keep to these rules, and one draw needn't show every extreme that they name: `tile_counts`: the tile counts sum to 12; the largest is exactly 7. `image_slots`: image slots and text slots together name every stream position once; each image's rows lie in order at consecutive positions. `text_slots`: see image_slots; text slots increase.
All inputs are finite; a program needn't handle non-finite values.
Results may differ from a plain program's by a relative error of at most 0.022.
The roundings to bfloat16 on the way count: a program that leaves them out, or rounds other values in their place, can miss the bound.
Values may be sent and summed in bfloat16 or wider, within the bound.
No kernel may reach another device: no remote copies, remote signals or barrier semaphores. Data moves between devices by JAX's collectives and lax.ppermute only.
A program may use at most 192 MiB of HBM per device.

v0:
```python
import jax
import jax.numpy as jnp
from jax import lax
from jax.sharding import PartitionSpec as P

HD = 128
SIDE = 32


def image_of(index_rows, tile_counts):
    bounds = jnp.cumsum(tile_counts) * (SIDE * SIDE)
    return jnp.sum((index_rows[:, None] >= bounds[None, :]).astype(jnp.int32), axis=1)


def shuffle_rows(values):
    row_count, width = values.shape
    grouped = values.reshape(row_count // (2 * SIDE), 2, SIDE // 2, 2, width)
    return grouped.transpose(0, 2, 4, 1, 3).reshape(row_count // 4, 4 * width)


def per_device(
    patches,
    norm_gain,
    query_weight,
    key_weight,
    value_weight,
    out_weight,
    layer_scale,
    merge_gain,
    merge_bias,
    proj_weight,
    proj_bias,
    text_rows,
    stream_gain,
    tile_counts,
    image_slots,
    text_slots,
):
    seq_index = lax.axis_index("seq")
    hid_index = lax.axis_index("hid")
    local_rows = patches.shape[0]
    local_heads = query_weight.shape[1] // HD
    tokens_f = patches.astype(jnp.float32)
    normed_in = (
        tokens_f * lax.rsqrt(jnp.mean(tokens_f * tokens_f, -1, keepdims=True) + 1e-06) * norm_gain
    ).astype(jnp.bfloat16)
    queries = (
        jnp.dot(normed_in, query_weight, preferred_element_type=jnp.float32) * HD ** (-0.5)
    ).astype(jnp.bfloat16)
    key_rows = jnp.dot(normed_in, key_weight, preferred_element_type=jnp.float32).astype(
        jnp.bfloat16
    )
    value_rows = jnp.dot(normed_in, value_weight, preferred_element_type=jnp.float32).astype(
        jnp.bfloat16
    )
    query_heads = queries.reshape(local_rows, local_heads, HD)
    query_ids = image_of(
        seq_index * local_rows + jnp.arange(local_rows, dtype=jnp.int32), tile_counts
    )

    def fold_block(state_now, key_block, value_block, block_start):
        maxima, totals, accumulated = state_now
        row_count = key_block.shape[0]
        key_heads = key_block.reshape(row_count, local_heads, HD)
        value_heads = value_block.reshape(row_count, local_heads, HD)
        scores = jnp.einsum(
            "qhd,khd->hqk", query_heads, key_heads, preferred_element_type=jnp.float32
        )
        key_ids = image_of(block_start + jnp.arange(row_count, dtype=jnp.int32), tile_counts)
        same_image = (query_ids[:, None] == key_ids[None, :])[None]
        scores = jnp.where(same_image, scores, jnp.float32(-1e30))
        new_max = jnp.maximum(maxima, jnp.max(scores, axis=-1))
        factor = jnp.exp(maxima - new_max)
        weights = jnp.where(same_image, jnp.exp(scores - new_max[..., None]), jnp.float32(0.0))
        totals = totals * factor + jnp.sum(weights, axis=-1)
        update = jnp.einsum(
            "hqk,khd->hqd",
            weights.astype(jnp.bfloat16),
            value_heads,
            preferred_element_type=jnp.float32,
        )
        accumulated = accumulated * factor[..., None] + update
        return (new_max, totals, accumulated)

    start_state = (
        jnp.full((local_heads, local_rows), -1e30, jnp.float32),
        jnp.zeros((local_heads, local_rows), jnp.float32),
        jnp.zeros((local_heads, local_rows, HD), jnp.float32),
    )
    key_piece = lax.all_gather(key_rows, "seq", axis=0, tiled=True)
    value_piece = lax.all_gather(value_rows, "seq", axis=0, tiled=True)
    row_count = key_piece.shape[0]
    block_rows = 512
    steps_count = row_count // block_rows
    key_blocks = key_piece.reshape(steps_count, block_rows, key_piece.shape[1])
    value_blocks = value_piece.reshape(steps_count, block_rows, value_piece.shape[1])

    def step_fn(state_in, inputs):
        key_block, value_block, index_now = inputs
        return (fold_block(state_in, key_block, value_block, index_now * block_rows), None)

    result, unused = lax.scan(
        step_fn, start_state, (key_blocks, value_blocks, jnp.arange(steps_count, dtype=jnp.int32))
    )
    maxima, totals, accumulated = result
    attended = (accumulated / totals[..., None]).astype(jnp.bfloat16)
    attended = attended.transpose(1, 0, 2).reshape(local_rows, local_heads * HD)
    branch_part = jnp.dot(attended, out_weight, preferred_element_type=jnp.float32)
    branch = lax.psum(branch_part.astype(jnp.bfloat16), "hid").astype(jnp.float32)
    merged = shuffle_rows(tokens_f + layer_scale * branch)
    mean_row = jnp.mean(merged, -1, keepdims=True)
    var_row = jnp.mean(merged * merged, -1, keepdims=True) - mean_row * mean_row
    block_width = merged.shape[1] // lax.axis_size("hid")
    merged_block = lax.dynamic_slice_in_dim(merged, hid_index * block_width, block_width, 1)
    merged_normed = (
        (merged_block - mean_row) * lax.rsqrt(var_row + 1e-05) * merge_gain + merge_bias
    ).astype(jnp.bfloat16)
    partial_proj = jnp.dot(
        lax.all_gather(merged_normed, "seq", axis=0, tiled=True),
        proj_weight,
        preferred_element_type=jnp.float32,
    )
    stream_size = image_slots.shape[0] + text_slots.shape[0]
    summed = lax.psum(partial_proj.astype(jnp.bfloat16), "hid").astype(jnp.float32)
    image_rows = jax.nn.gelu(summed + proj_bias, approximate=False).astype(jnp.bfloat16)
    stream_cols = (
        jnp.zeros((stream_size, image_rows.shape[1]), jnp.bfloat16)
        .at[image_slots]
        .set(image_rows)
        .at[text_slots]
        .set(text_rows)
    )
    stream_full = lax.all_to_all(stream_cols, "seq", split_axis=0, concat_axis=1, tiled=True)
    stream_f = stream_full.astype(jnp.float32)
    inverse_rms = lax.rsqrt(jnp.mean(stream_f * stream_f, -1, keepdims=True) + 1e-05)
    out_width = stream_full.shape[1] // lax.axis_size("hid")
    stream_share = lax.dynamic_slice_in_dim(stream_full, hid_index * out_width, out_width, 1)
    normed_share = (stream_share.astype(jnp.float32) * inverse_rms * stream_gain).astype(
        jnp.bfloat16
    )
    return (stream_share, normed_share)


def solution(mesh):
    return jax.shard_map(
        per_device,
        mesh=mesh,
        in_specs=(
            P("seq", None),
            P(),
            P(None, "hid"),
            P(None, "hid"),
            P(None, "hid"),
            P("hid", None),
            P(),
            P("hid"),
            P("hid"),
            P("hid", "seq"),
            P("seq"),
            P(None, "seq"),
            P("hid"),
            P(),
            P(),
            P(),
        ),
        out_specs=(P("seq", "hid"), P("seq", "hid")),
        check_vma=False,
    )
```

profile of v0, /device:TPU:0, one launch (start us, length us, event | category | flops | bytes accessed | tf_op | source)
XLA Modules:
  0.0 976.0 jit_solution(10442808038477700343)
XLA Ops:
  9.8 4.2 convolution_convert_fusion.3
  14.1 5.0 convolution_convert_fusion.2
  19.2 4.2 fusion.32
  24.6 54.9 %all-gather.4.cloned.1.call-done = bf16[12288,512]{1,0:T(8,128)(2,1)} async-done(((bf16[384,512]{1,0:T(8,128)(2,1)}), bf16[12288,512]{1,0:T(8,128)(2,1)}) %all-gather.4.cloned.1.call-update) | async-done | bytes 12582928 | tf_op jit(solution)/shard_map/all_gather | solution.py:90
  79.5 64.6 %all-gather.6.cloned.1.call-done = bf16[12288,512]{1,0:T(8,128)(2,1)} async-done(((bf16[384,512]{1,0:T(8,128)(2,1)}), bf16[12288,512]{1,0:T(8,128)(2,1)}) %all-gather.6.cloned.1.call-update) | async-done | bytes 12582928 | tf_op jit(solution)/shard_map/all_gather | solution.py:91
  144.1 443.7 %while.17 = (s32[]{:T(128)}, f32[4,384]{1,0:T(4,128)S(1)}, f32[4,384]{1,0:T(4,128)S(1)}, f32[4,384,128]{2,1,0:T(8,128)}, s32[384]{0:T(512)S(1)}, /*index=5*/s32[...) while((s32[]{:T(128)}, f32[4,384]{1,0:T(4,128)S(1)}, ...), condition=%wide.region_7.8_spmd.clone, body=%wide.region_3.7_spmd.clone.sunk | while | flops 411316224 | bytes 17540812 | solution.py:102
  150.0 3.6 fusion.60
  158.4 4.0 fusion.63
  168.3 3.6 fusion.60
  176.6 4.3 fusion.63
  186.8 3.6 fusion.60
  195.1 4.3 fusion.63
  205.3 3.6 fusion.60
  213.6 4.3 fusion.63
  223.8 3.6 fusion.60
  232.1 4.3 fusion.63
  242.3 3.6 fusion.60
  250.6 4.3 fusion.63
  260.8 3.6 fusion.60
  269.1 4.3 fusion.63
  279.3 3.6 fusion.60
  287.6 4.3 fusion.63
  297.8 3.6 fusion.60
  306.1 4.3 fusion.63
  316.3 3.6 fusion.60
  324.6 4.3 fusion.63
  334.8 3.6 fusion.60
  343.1 4.3 fusion.63
  361.6 4.3 fusion.63
  371.8 3.6 fusion.60
  380.1 4.3 fusion.63
  398.6 4.3 fusion.63
  408.7 3.6 fusion.60
  417.1 4.3 fusion.63
  427.2 3.6 fusion.60
  435.6 4.3 fusion.63
  445.7 3.6 fusion.60
  454.1 4.3 fusion.63
  464.2 3.6 fusion.60
  472.6 4.3 fusion.63
  482.7 3.6 fusion.60
  491.1 4.3 fusion.63
  501.2 3.6 fusion.60
  509.6 4.3 fusion.63
  519.7 3.6 fusion.60
  528.1 4.3 fusion.63
  546.6 4.3 fusion.63
  556.7 3.6 fusion.60
  565.1 4.3 fusion.63
  575.2 3.6 fusion.60
  583.6 4.3 fusion.63
  594.5 64.3 %all-reduce.3.cloned.1.call-done = bf16[384,3200]{1,0:T(8,128)(2,1)} async-done(((bf16[384,3200]{1,0:T(8,128)(2,1)}), bf16[384,3200]{1,0:T(8,128)(2,1)}) %all-reduce.3.cloned.1.call-update) | async-done | bytes 2457616 | tf_op jit(solution)/shard_map/psum | solution.py:109
  658.9 4.5 convert_add_fusion
  663.4 6.8 reshape.161
  670.2 39.8 %copy.71 = f32[6,2,16,2,3200]{2,0,3,1,4:T(8,128)} copy(f32[6,2,16,2,3200]{4,3,2,1,0:T(2,128)} %reshape.161) | data formatting | bytes 9830400 | tf_op jit(solution)/shard_map/reshape | solution.py:17
  709.9 17.3 %bitcast_reduce_fusion = (f32[6,16]{1,0:T(8,128)S(1)}, f32[6,16]{1,0:T(8,128)S(1)}) fusion(f32[6,2,16,2,3200]{2,0,3,1,4:T(8,128)} %copy.71), kind=kLoop, calls=%fused_computation.81 | loop fusion | flops 3686208 | bytes 4915968 | tf_op jit(solution)/shard_map/reduce_sum | solution.py:111
  727.4 31.2 %reshape.162 = f32[96,12800]{0,1:T(8,128)} reshape(f32[6,16,3200,2,2]{1,0,4,3,2:T(8,128)} %bitcast.71) | data formatting | bytes 9830400 | tf_op jit(solution)/shard_map/reshape | solution.py:18
  761.8 78.9 %all-gather.8.cloned.1.call-done = bf16[3072,3200]{1,0:T(8,128)(2,1)} async-done(((bf16[96,3200]{1,0:T(8,128)(2,1)}), bf16[3072,3200]{1,0:T(8,128)(2,1)}) %all-gather.8.cloned.1.call-update) | async-done | bytes 19660816 | tf_op jit(solution)/shard_map/all_gather | solution.py:119
  840.7 14.4 %convolution_convert_fusion.1 = bf16[3072,192]{0,1:T(8,128)(2,1)} fusion(bf16[3072,3200]{1,0:T(8,128)(2,1)} %all-gather.8.cloned.1.call-done, bf16[3200,192]{0,1:T(8,128)(2,1)} %param.27), kind=kOutput, calls=%fused_computation.34 | convolution fusion | flops 3775463424 | bytes 22069248 | tf_op jit(solution)/shard_map/dot_general | solution.py:118
  855.3 46.3 %all-reduce.5.cloned.1.call-done = bf16[3072,192]{0,1:T(8,128)(2,1)} async-done(((bf16[3072,192]{0,1:T(8,128)(2,1)}), bf16[3072,192]{0,1:T(8,128)(2,1)}) %all-reduce.5.cloned.1.call-update) | async-done | bytes 1179664 | tf_op jit(solution)/shard_map/psum | solution.py:124
  901.6 6.4 fusion.20
  909.6 14.5 %scatter_custom_fusion = bf16[3584,192]{1,0:T(8,128)(2,1)S(1)} fusion(s32[3072]{0:T(1024)S(1)} %compare_select_fusion, bf16[3072,192]{1,0:T(8,128)(2,1)} %copy.73, bf16[]{:T(256)} %constant.65.clone.1), kind=kCustom, calls=%fused_computation.64 | custom fusion | bytes 1376768 | tf_op jit(solution)/shard_map/scatter | solution.py:129
  930.0 7.3 all-to-all-start
  937.4 23.9 %all-to-all-done = bf16[32,112,192]{1,2,0:T(8,128)(2,1)} async-done(((bf16[32,112,192]{1,2,0:T(8,128)(2,1)}), bf16[32,112,192]{1,2,0:T(8,128)(2,1)}, u32[]{:S(2)}, u32[]{:S(2)}) %all-to-all-start) | async-done | bytes 1376288 | tf_op jit(solution)/shard_map/all_to_all | solution.py:133
  (361 shorter events, 278.7 us)
Async XLA Ops:
  7.2 584.1 %copy-start = (bf16[512,3200]{1,0:T(8,128)(2,1)S(1)}, bf16[512,3200]{1,0:T(8,128)(2,1)}, u32[]{:S(2)}) copy-start(bf16[512,3200]{1,0:T(8,128)(2,1)} %param.23) | copy-start | bytes 9830404
  7.2 72.3 %all-gather.4.cloned.1.call-start = ((), (), s32[]{:S(2)}) async-start(), calls=%async_computation.1 | async-start | bytes 12976128 | tf_op jit(solution)/shard_map/all_gather | solution.py:90
  7.2 2.6 copy-start.2
  9.8 4.3 copy-start.12
  14.1 130.0 %all-gather.6.cloned.1.call-start = ((), (), s32[]{:S(2)}) async-start(), calls=%async_computation.2 | async-start | bytes 12976128 | tf_op jit(solution)/shard_map/all_gather | solution.py:91
  19.2 639.7 %all-reduce.3.cloned.1.call-start = ((), (), s32[]{:S(2)}) async-start(), calls=%async_computation.3 | async-start | bytes 4915200 | tf_op jit(solution)/shard_map/psum | solution.py:109
  19.2 5.1 copy-start.13
  591.3 67.6 %copy-start.5 = (f32[3200]{0:T(1024)S(1)}, f32[3200]{0:T(1024)}, u32[]{:S(2)}) copy-start(f32[3200]{0:T(1024)} %param.24) | copy-start | bytes 38404
  594.3 64.6 %copy-start.3 = (bf16[384,3200]{1,0:T(8,128)(2,1)S(1)}, bf16[384,3200]{1,0:T(8,128)(2,1)}, u32[]{:S(2)}) copy-start(bf16[384,3200]{1,0:T(8,128)(2,1)} %param.18) | copy-start | bytes 7372804
  594.3 246.4 %all-gather.8.cloned.1.call-start = ((), (), s32[]{:S(2)}) async-start(), calls=%async_computation.4 | async-start | bytes 20275200 | tf_op jit(solution)/shard_map/all_gather | solution.py:119
  758.5 2.1 copy-start.6
  758.5 2.1 copy-start.7
  761.7 93.4 %copy-start.4 = (bf16[512,192]{0,1:T(8,128)(2,1)S(1)}, bf16[512,192]{0,1:T(8,128)(2,1)}, u32[]{:S(2)}) copy-start(bf16[512,192]{0,1:T(8,128)(2,1)} %param.29) | copy-start | bytes 589828
  761.8 93.6 %copy-start.10 = (s32[512]{0:T(512)S(1)}, s32[512]{0:T(512)}, u32[]{:S(2)}) copy-start(s32[512]{0:T(512)} %param.33) | copy-start | bytes 6148
  761.8 93.6 %copy-start.8 = (s32[3072]{0:T(1024)S(1)}, s32[3072]{0:T(1024)}, u32[]{:S(2)}) copy-start(s32[3072]{0:T(1024)} %param.32) | copy-start | bytes 36868
  761.8 139.8 %copy-start.11 = (f32[192]{0:T(256)S(1)}, f32[192]{0:T(256)}, u32[]{:S(2)}) copy-start(f32[192]{0:T(256)} %param.28) | copy-start | bytes 2308
  761.8 139.8 %all-reduce.5.cloned.1.call-start = ((), (), s32[]{:S(2)}) async-start(), calls=%async_computation.5 | async-start | bytes 2359296 | tf_op jit(solution)/shard_map/psum | solution.py:124
  930.0 33.5 %copy-start.9 = (f32[1536]{0:T(1024)S(1)}, f32[1536]{0:T(1024)}, u32[]{:S(2)}) copy-start(f32[1536]{0:T(1024)} %param.30) | copy-start | bytes 18436
  930.0 31.3 %all-to-all-start = ((bf16[32,112,192]{1,2,0:T(8,128)(2,1)}), bf16[32,112,192]{1,2,0:T(8,128)(2,1)}, u32[]{:S(2)}, u32[]{:S(2)}) async-start(bf16[32,112,192]{1,2,0:T(8,128)(2,1)} %copy.76), calls=%async_computation | async-start | bytes 3145728 | tf_op jit(solution)/shard_map/all_to_all | solution.py:133
  937.4 32.1 %copy-start.1 = (bf16[512,3200]{1,0:T(8,128)(2,1)S(1)}, bf16[512,3200]{1,0:T(8,128)(2,1)}, u32[]{:S(2)}) copy-start(bf16[512,3200]{1,0:T(8,128)(2,1)} %param.23) | copy-start | bytes 9830404
Sparse Core Ops, SparseCore 0:
  14.2 65.2 all-gather.3
  81.7 62.3 all-gather.5
  594.4 64.4 all-reduce.2
  761.9 78.7 all-gather.7
  855.3 46.2 all-reduce.4
where the time goes:
time: 982 us; the launch traced here: 976 us
  waiting for transfers between devices  333 us (34%)
  local copies, waits for them, and re-layouts  279 us (28%)
  matrix products  220 us (22%)
  other arithmetic  106 us (11%)
  loops' own time  16.4 us (2%)
  between operations  14 us (1%)
    dynamic_slice x96, local copies, waits for them, and re-layouts, per_device(): lax.scan(step_fn, start_state, (key_blocks, value_blocks, jnp.arange(step...  169 us
    dot_general x24, matrix products, fold_block(): jnp.einsum('hqk,khd->hqd', weights.astype(jnp.bfloat16), value_heads, pre...  102 us
    dot_general x24, matrix products, fold_block(): jnp.einsum('qhd,khd->hqk', query_heads, key_heads, preferred_element_type...  87.1 us
    all_gather x1, waiting for transfers between devices, per_device(): lax.all_gather(merged_normed, 'seq', axis=0, tiled=True)  78.9 us
    all_gather x1, waiting for transfers between devices, per_device(): value_piece = lax.all_gather(value_rows, 'seq', axis=0, tiled=True)  64.6 us
    psum x1, waiting for transfers between devices, per_device(): lax.psum(branch_part.astype(jnp.bfloat16), 'hid').astype(jnp.float32)  64.3 us
    reduce_sum x24, other arithmetic, fold_block(): totals = totals * factor + jnp.sum(weights, axis=-1)  61.6 us
    all_gather x1, waiting for transfers between devices, per_device(): key_piece = lax.all_gather(key_rows, 'seq', axis=0, tiled=True)  54.9 us
  transfers between devices with their start and end apart: 6, of which 6 were waited for; matrix products, arithmetic and copies ran while one was open for 1% of the time, Pallas kernels for 0%

commit v1 on v0

--- a/solution.py
+++ b/solution.py
@@ -88,7 +88,11 @@
         jnp.zeros((local_heads, local_rows, HD), jnp.float32),
     )
     key_piece = lax.all_gather(key_rows, "seq", axis=0, tiled=True)
-    value_piece = lax.all_gather(value_rows, "seq", axis=0, tiled=True)
+    n_blocks = lax.axis_size("seq")
+    rack = [n_blocks if u == 0 else 1 for u in range(value_rows.ndim)]
+    value_piece = lax.all_to_all(
+        jnp.tile(value_rows, rack), "seq", split_axis=0, concat_axis=0, tiled=True
+    )
     row_count = key_piece.shape[0]
     block_rows = 512
     steps_count = row_count // block_rows

time: 982 us -> 1050 us (1.069)
  waiting for transfers between devices: 333 us -> 386 us
    all_to_all x0 -> x1, waiting for transfers between devices: none -> 171 us  [per_device(): lax.all_to_all(jnp.tile(value_rows, rack), 'seq', split_axis=0, concat_ax...]
    all_gather x1 -> x0, waiting for transfers between devices: 64.6 us -> none  [per_device(): value_piece = lax.all_gather(value_rows, 'seq', axis=0, tiled=True)]
    all_gather x1, waiting for transfers between devices: 54.9 us -> 0.01 us  [per_device(): key_piece = lax.all_gather(key_rows, 'seq', axis=0, tiled=True)]
  transfers between devices with their start and end apart: 6 -> 6, of which waited for: 6 -> 5; matrix products, arithmetic and copies ran while one was open for 1% -> 2% of each run, Pallas kernels for 0% -> 0%
where the time goes in v1:
time: 1050 us; the launch traced here: 1040 us
  waiting for transfers between devices  386 us (37%)
  local copies, waits for them, and re-layouts  283 us (27%)
  matrix products  220 us (21%)
  other arithmetic  106 us (10%)
  loops' own time  16.4 us (2%)
  starting transfers between devices  15.2 us (1%)
  between operations  14 us (1%)
    all_to_all x1, waiting for transfers between devices, per_device(): lax.all_to_all(jnp.tile(value_rows, rack), 'seq', split_axis=0, concat_ax...  171 us
    dynamic_slice x96, local copies, waits for them, and re-layouts, per_device(): lax.scan(step_fn, start_state, (key_blocks, value_blocks, jnp.arange(step...  168 us
    dot_general x24, matrix products, fold_block(): jnp.einsum('hqk,khd->hqd', weights.astype(jnp.bfloat16), value_heads, pre...  102 us
    dot_general x24, matrix products, fold_block(): jnp.einsum('qhd,khd->hqk', query_heads, key_heads, preferred_element_type...  87.5 us
    all_gather x1, waiting for transfers between devices, per_device(): lax.all_gather(merged_normed, 'seq', axis=0, tiled=True)  78.9 us
    psum x1, waiting for transfers between devices, per_device(): lax.psum(branch_part.astype(jnp.bfloat16), 'hid').astype(jnp.float32)  65.7 us
    reduce_sum x24, other arithmetic, fold_block(): totals = totals * factor + jnp.sum(weights, axis=-1)  61.6 us
    reshape x2, local copies, waits for them, and re-layouts, shuffle_rows(): grouped = values.reshape(row_count // (2 * SIDE), 2, SIDE // 2, 2, width)  46.5 us
  transfers between devices with their start and end apart: 6, of which 5 were waited for; matrix products, arithmetic and copies ran while one was open for 2% of the time, Pallas kernels for 0%

profile of v1, /device:TPU:0, one launch (start us, length us, event | category | flops | bytes accessed | tf_op | source)
XLA Modules:
  0.0 1040.6 jit_solution(4683728854000141110)
XLA Ops:
  9.8 4.2 convolution_convert_fusion.3
  14.1 4.2 convolution_convert_fusion.2
  18.3 6.0 tile.2
  24.3 7.5 all-to-all-start
  31.9 4.3 fusion.32
  37.4 171.3 %all-to-all-done = bf16[32,384,512]{2,1,0:T(8,128)(2,1)} async-done(((bf16[32,384,512]{2,1,0:T(8,128)(2,1)}), bf16[32,384,512]{2,1,0:T(8,128)(2,1)}, u32[]{:S(2)}, u32[]{:S(2)}) %all-to-all-start) | async-done | bytes 12582944 | tf_op jit(solution)/shard_map/all_to_all | solution.py:93
  208.7 442.4 %while.17 = (s32[]{:T(128)}, f32[4,384]{1,0:T(4,128)S(1)}, f32[4,384]{1,0:T(4,128)S(1)}, f32[4,384,128]{2,1,0:T(8,128)}, s32[384]{0:T(512)S(1)}, /*index=5*/s32[...) while((s32[]{:T(128)}, f32[4,384]{1,0:T(4,128)S(1)}, ...), condition=%wide.region_7.8_spmd.clone, body=%wide.region_3.7_spmd.clone.sunk | while | flops 411316224 | bytes 17540812 | solution.py:106
  214.6 3.6 fusion.60
  222.9 4.0 fusion.63
  232.8 3.6 fusion.60
  241.1 4.3 fusion.63
  251.2 3.6 fusion.60
  259.5 4.3 fusion.63
  269.6 3.6 fusion.60
  278.0 4.3 fusion.63
  288.1 3.6 fusion.60
  296.4 4.3 fusion.63
  306.5 3.6 fusion.60
  314.8 4.3 fusion.63
  325.0 3.6 fusion.60
  333.3 4.3 fusion.63
  343.4 3.6 fusion.60
  351.7 4.3 fusion.63
  361.9 3.6 fusion.60
  370.2 4.3 fusion.63
  380.3 3.6 fusion.60
  388.6 4.3 fusion.63
  398.7 3.6 fusion.60
  407.1 4.3 fusion.63
  417.2 3.6 fusion.60
  425.5 4.3 fusion.63
  435.6 3.6 fusion.60
  443.9 4.3 fusion.63
  454.1 3.6 fusion.60
  462.4 4.3 fusion.63
  472.5 3.6 fusion.60
  480.8 4.3 fusion.63
  491.0 3.6 fusion.60
  499.3 4.3 fusion.63
  509.4 3.6 fusion.60
  517.7 4.3 fusion.63
  527.8 3.6 fusion.60
  536.2 4.3 fusion.63
  546.3 3.6 fusion.60
  554.6 4.3 fusion.63
  564.7 3.6 fusion.60
  573.0 4.3 fusion.63
  591.5 4.3 fusion.63
  609.9 4.3 fusion.63
  628.4 4.3 fusion.63
  646.8 4.3 fusion.63
  657.8 65.7 %all-reduce.3.cloned.1.call-done = bf16[384,3200]{1,0:T(8,128)(2,1)} async-done(((bf16[384,3200]{1,0:T(8,128)(2,1)}), bf16[384,3200]{1,0:T(8,128)(2,1)}) %all-reduce.3.cloned.1.call-update) | async-done | bytes 2457616 | tf_op jit(solution)/shard_map/psum | solution.py:113
  723.6 4.5 convert_add_fusion
  728.1 6.7 reshape.169
  734.8 39.8 %copy.84 = f32[6,2,16,2,3200]{2,0,3,1,4:T(8,128)} copy(f32[6,2,16,2,3200]{4,3,2,1,0:T(2,128)} %reshape.169) | data formatting | bytes 9830400 | tf_op jit(solution)/shard_map/reshape | solution.py:17
  774.6 17.3 %bitcast_reduce_fusion = (f32[6,16]{1,0:T(8,128)S(1)}, f32[6,16]{1,0:T(8,128)S(1)}) fusion(f32[6,2,16,2,3200]{2,0,3,1,4:T(8,128)} %copy.84), kind=kLoop, calls=%fused_computation.81 | loop fusion | flops 3686208 | bytes 4915968 | tf_op jit(solution)/shard_map/reduce_sum | solution.py:115
  792.0 31.2 %reshape.170 = f32[96,12800]{0,1:T(8,128)} reshape(f32[6,16,3200,2,2]{1,0,4,3,2:T(8,128)} %bitcast.71) | data formatting | bytes 9830400 | tf_op jit(solution)/shard_map/reshape | solution.py:18
  826.5 78.9 %all-gather.5.cloned.1.call-done = bf16[3072,3200]{1,0:T(8,128)(2,1)} async-done(((bf16[96,3200]{1,0:T(8,128)(2,1)}), bf16[3072,3200]{1,0:T(8,128)(2,1)}) %all-gather.5.cloned.1.call-update) | async-done | bytes 19660816 | tf_op jit(solution)/shard_map/all_gather | solution.py:123
  905.4 14.4 %convolution_convert_fusion.1 = bf16[3072,192]{0,1:T(8,128)(2,1)} fusion(bf16[3072,3200]{1,0:T(8,128)(2,1)} %all-gather.5.cloned.1.call-done, bf16[3200,192]{0,1:T(8,128)(2,1)} %param.27), kind=kOutput, calls=%fused_computation.34 | convolution fusion | flops 3775463424 | bytes 22069248 | tf_op jit(solution)/shard_map/dot_general | solution.py:122
  920.0 46.2 %all-reduce.5.cloned.1.call-done = bf16[3072,192]{0,1:T(8,128)(2,1)} async-done(((bf16[3072,192]{0,1:T(8,128)(2,1)}), bf16[3072,192]{0,1:T(8,128)(2,1)}) %all-reduce.5.cloned.1.call-update) | async-done | bytes 1179664 | tf_op jit(solution)/shard_map/psum | solution.py:128
  966.3 6.4 fusion.20
  974.3 14.5 %scatter_custom_fusion = bf16[3584,192]{1,0:T(8,128)(2,1)S(1)} fusion(s32[3072]{0:T(1024)S(1)} %compare_select_fusion, bf16[3072,192]{1,0:T(8,128)(2,1)} %copy.86, bf16[]{:T(256)} %constant.65.clone.1), kind=kCustom, calls=%fused_computation.64 | custom fusion | bytes 1376768 | tf_op jit(solution)/shard_map/scatter | solution.py:133
  994.7 7.3 all-to-all-start.1
  1002.1 23.9 %all-to-all-done.1 = bf16[32,112,192]{1,2,0:T(8,128)(2,1)} async-done(((bf16[32,112,192]{1,2,0:T(8,128)(2,1)}), bf16[32,112,192]{1,2,0:T(8,128)(2,1)}, u32[]{:S(2)}, u32[]{:S(2)}) %all-to-all-start.1) | async-done | bytes 1376288 | tf_op jit(solution)/shard_map/all_to_all | solution.py:137
  (361 shorter events, 280.5 us)
Async XLA Ops:
  7.2 647.4 %copy-start = (bf16[512,3200]{1,0:T(8,128)(2,1)S(1)}, bf16[512,3200]{1,0:T(8,128)(2,1)}, u32[]{:S(2)}) copy-start(bf16[512,3200]{1,0:T(8,128)(2,1)} %param.23) | copy-start | bytes 9830404
  7.2 201.5 %all-gather.3.cloned.1.call-start = ((), (), s32[]{:S(2)}) async-start(), calls=%async_computation.2 | async-start | bytes 12976128 | tf_op jit(solution)/shard_map/all_gather | solution.py:90
  7.2 2.6 copy-start.2
  9.8 4.3 copy-start.12
  24.3 184.4 %all-to-all-start = ((bf16[32,384,512]{2,1,0:T(8,128)(2,1)}), bf16[32,384,512]{2,1,0:T(8,128)(2,1)}, u32[]{:S(2)}, u32[]{:S(2)}) async-start(bf16[32,384,512]{2,1,0:T(8,128)(2,1)} %tile.2), calls=%async_computation | async-start | bytes 25165824 | tf_op jit(solution)/shard_map/all_to_all | solution.py:93
  31.8 691.8 %all-reduce.3.cloned.1.call-start = ((), (), s32[]{:S(2)}) async-start(), calls=%async_computation.3 | async-start | bytes 4915200 | tf_op jit(solution)/shard_map/psum | solution.py:113
  31.9 5.2 copy-start.13
  654.6 69.0 %copy-start.5 = (f32[3200]{0:T(1024)S(1)}, f32[3200]{0:T(1024)}, u32[]{:S(2)}) copy-start(f32[3200]{0:T(1024)} %param.24) | copy-start | bytes 38404
  657.6 66.0 %copy-start.3 = (bf16[384,3200]{1,0:T(8,128)(2,1)S(1)}, bf16[384,3200]{1,0:T(8,128)(2,1)}, u32[]{:S(2)}) copy-start(bf16[384,3200]{1,0:T(8,128)(2,1)} %param.18) | copy-start | bytes 7372804
  657.6 247.8 %all-gather.5.cloned.1.call-start = ((), (), s32[]{:S(2)}) async-start(), calls=%async_computation.4 | async-start | bytes 20275200 | tf_op jit(solution)/shard_map/all_gather | solution.py:123
  823.2 2.1 copy-start.6
  823.2 2.1 copy-start.7
  826.4 93.4 %copy-start.4 = (bf16[512,192]{0,1:T(8,128)(2,1)S(1)}, bf16[512,192]{0,1:T(8,128)(2,1)}, u32[]{:S(2)}) copy-start(bf16[512,192]{0,1:T(8,128)(2,1)} %param.29) | copy-start | bytes 589828
  826.4 93.6 %copy-start.10 = (s32[512]{0:T(512)S(1)}, s32[512]{0:T(512)}, u32[]{:S(2)}) copy-start(s32[512]{0:T(512)} %param.33) | copy-start | bytes 6148
  826.4 93.6 %copy-start.8 = (s32[3072]{0:T(1024)S(1)}, s32[3072]{0:T(1024)}, u32[]{:S(2)}) copy-start(s32[3072]{0:T(1024)} %param.32) | copy-start | bytes 36868
  826.5 139.8 %copy-start.11 = (f32[192]{0:T(256)S(1)}, f32[192]{0:T(256)}, u32[]{:S(2)}) copy-start(f32[192]{0:T(256)} %param.28) | copy-start | bytes 2308
  826.5 139.8 %all-reduce.5.cloned.1.call-start = ((), (), s32[]{:S(2)}) async-start(), calls=%async_computation.5 | async-start | bytes 2359296 | tf_op jit(solution)/shard_map/psum | solution.py:128
  994.7 33.5 %copy-start.9 = (f32[1536]{0:T(1024)S(1)}, f32[1536]{0:T(1024)}, u32[]{:S(2)}) copy-start(f32[1536]{0:T(1024)} %param.30) | copy-start | bytes 18436
  994.7 31.3 %all-to-all-start.1 = ((bf16[32,112,192]{1,2,0:T(8,128)(2,1)}), bf16[32,112,192]{1,2,0:T(8,128)(2,1)}, u32[]{:S(2)}, u32[]{:S(2)}) async-start(bf16[32,112,192]{1,2,0:T(8,128)(2,1)} %copy.89), calls=%async_computation.1 | async-start | bytes 3145728 | tf_op jit(solution)/shard_map/all_to_all | solution.py:137
  1002.0 32.0 %copy-start.1 = (bf16[512,3200]{1,0:T(8,128)(2,1)S(1)}, bf16[512,3200]{1,0:T(8,128)(2,1)}, u32[]{:S(2)}) copy-start(bf16[512,3200]{1,0:T(8,128)(2,1)} %param.23) | copy-start | bytes 9830404
Sparse Core Ops, SparseCore 0:
  14.2 190.0 all-gather.2
  657.7 65.8 all-reduce.2
  826.5 78.7 all-gather.4
  920.0 46.2 all-reduce.4
